TPU v7x, 32 devices: a whole 2x2x4 slice. The times are simulated.
32 devices in a mesh: row: 8 (over y, x, core), col: 4 (over z).
Axes of the slice: x: 2, y: 2, z: 4, core: 2. Of those that a mesh axis runs over, the one named last changes fastest.
Arguments:
- final_amp: bfloat16 [8, 32, 128, 440], P('row', 'col'), may hold values from -0.19921875 to 0.19921875
- initial_amp: bfloat16 [4, 32, 128, 440], P('col', 'row'), may hold values from -0.19921875 to 0.19921875
- pair_final: int32 [8, 4, 128], P('row', 'col'), may hold values from 0 to 31
- pair_initial: int32 [8, 4, 128], P('row', 'col'), may hold values from 0 to 31
- map_final: int32 [8, 32, 440], P('row', 'col'), may hold values from 0 to 439, each once within a row
- map_initial: int32 [4, 32, 440], P('col', 'row'), may hold values from 0 to 439, each once within a row
- counts: int32 [8, 4], P('row', 'col'), may hold values from 16 to 128, as said below
Outputs:
- density: float32 [440, 440], replicated
Inputs may be any that keep to these rules, and one draw needn't show every extreme that they name: `counts`: slots at or past a cell's count are ignored. Exactly one cell of every draw has 128 live slots.
All inputs are finite; a program needn't handle non-finite values.
Results may differ from a plain program's by a relative error of at most 0.0003.
Values may be sent and summed in bfloat16 or wider, within the bound.
A program may use at most 64 MiB of HBM per device.

v0:
```python
import jax
import jax.numpy as jnp
from jax import lax
from jax.sharding import PartitionSpec as P

GROUP = 32


def permute_columns(blocks, orbital_map):
    return jnp.take(blocks, orbital_map, axis=1)


def shards(final_amp, initial_amp, pair_final, pair_initial, map_final, map_initial, counts):
    own_final = jax.vmap(permute_columns)(final_amp[0], map_final[0])[None]
    own_initial = jax.vmap(permute_columns)(initial_amp[0], map_initial[0])[None]
    row_seg = lax.all_gather(own_final, "col", axis=1, tiled=True)[0]
    column_seg = lax.all_gather(own_initial, "row", axis=1, tiled=True)[0]
    slots_final = pair_final[0, 0]
    slots_initial = pair_initial[0, 0]
    live_count = counts[0, 0]
    orbitals = final_amp.shape[3]
    group_size = GROUP

    def advance(index, summed):
        first_slot = index * group_size
        which_final = lax.dynamic_slice_in_dim(slots_final, first_slot, group_size)
        which_initial = lax.dynamic_slice_in_dim(slots_initial, first_slot, group_size)
        live_mask = first_slot + jnp.arange(group_size, dtype=jnp.int32) < live_count
        left = jnp.take(row_seg, which_final, axis=0)
        right = jnp.take(column_seg, which_initial, axis=0)
        left = jnp.where(live_mask[:, None, None], left, jnp.zeros_like(left))
        product = lax.dot_general(
            left.reshape(-1, orbitals),
            right.reshape(-1, orbitals),
            (((0,), (0,)), ((), ())),
            preferred_element_type=jnp.float32,
        )
        return summed + product

    turns = (live_count + group_size - 1) // group_size
    partial_density = lax.fori_loop(0, turns, advance, jnp.zeros((orbitals, orbitals), jnp.float32))
    band = lax.psum_scatter(partial_density, "col", scatter_dimension=0, tiled=True)
    band = lax.psum(band, "row")
    density = lax.all_gather(band, "col", axis=0, tiled=True)
    return density


def solution(mesh):
    placed = (
        P("row", "col", None, None),
        P("col", "row", None, None),
        P("row", "col", None),
        P("row", "col", None),
        P("row", "col", None),
        P("col", "row", None),
        P("row", "col"),
    )
    return jax.shard_map(shards, mesh=mesh, in_specs=placed, out_specs=P(), check_vma=False)
```

profile of v0, /device:TPU:0, one launch (start us, length us, event | category | flops | bytes accessed | tf_op | source)
XLA Modules:
  0.0 322.3 jit_solution(12124861493017973160)
XLA Ops:
  6.5 0.8 fusion.18
  7.3 0.7 compare_and_fusion.2
  8.2 30.8 %gather_fusion.2 = bf16[3520,128]{1,0:T(8,128)(2,1)S(1)} fusion(bf16[8,128,440]{1,2,0:T(8,128)(2,1)S(1)} %bitcast.44, s32[3520]{0:T(1024)S(1)} %reshape.110), kind=kCustom, calls=%fused_computation.2 | custom fusion | bytes 1830400 | tf_op jit(solution)/shard_map/vmap(jit(_take))/gather | solution.py:10
  39.0 1.4 broadcast_select_fusion
  40.5 15.7 %gather_fusion.3 = bf16[1760,128]{1,0:T(8,128)(2,1)S(1)} fusion(bf16[4,128,440]{1,2,0:T(8,128)(2,1)S(1)} %bitcast.45, s32[1760]{0:T(1024)S(1)} %reshape.116), kind=kCustom, calls=%fused_computation.3 | custom fusion | bytes 915200 | tf_op jit(solution)/shard_map/vmap(jit(_take))/gather | solution.py:10
  56.3 1.1 broadcast_select_fusion.1
  58.2 56.1 %all-gather.4.cloned.1.call-done = bf16[1,32,128,440]{2,3,0,1:T(8,128)(2,1)} async-done(((bf16[1,8,128,440]{2,3,0,1:T(8,128)(2,1)}), bf16[1,32,128,440]{2,3,0,1:T(8,128)(2,1)}) %all-gather.4.cloned.1.call-update) | async-done | bytes 3604496 | tf_op jit(solution)/shard_map/all_gather | solution.py:16
  114.3 6.4 %copy.18 = bf16[32,128,440]{2,1,0:T(8,128)(2,1)} copy(bf16[32,128,440]{1,2,0:T(8,128)(2,1)} %bitcast.47) | data formatting | bytes 7208960 | tf_op jit(solution)/shard_map/while | solution.py:41
  120.7 28.2 %all-gather.6.cloned.1.call-done = bf16[1,32,128,440]{2,3,0,1:T(8,128)(2,1)} async-done(((bf16[1,4,128,440]{2,3,0,1:T(8,128)(2,1)}), bf16[1,32,128,440]{2,3,0,1:T(8,128)(2,1)}) %all-gather.6.cloned.1.call-update) | async-done | bytes 3604496 | tf_op jit(solution)/shard_map/all_gather | solution.py:17
  148.9 6.5 %copy.19 = bf16[32,128,440]{2,1,0:T(8,128)(2,1)} copy(bf16[32,128,440]{1,2,0:T(8,128)(2,1)} %bitcast.48) | data formatting | bytes 7208960 | tf_op jit(solution)/shard_map/while | solution.py:41
  155.3 0.1 broadcast_in_dim.43
  155.5 33.5 %while.10 = (s32[]{:T(128)}, f32[440,440]{1,0:T(8,128)S(1)}, s32[]{:T(128)}, s32[]{:T(128)}, s32[128]{0:T(128)S(1)}, /*index=5*/bf16[32,128,440]{2,1,0:T(8,128)(...) while((s32[]{:T(128)}, f32[440,440]{1,0:T(8,128)S(1)}, ...), condition=%wide.region_1.3_spmd, body=%wide.region_0.0_spmd.sunk | while | flops 1591574016 | bytes 23185264 | solution.py:41
  155.5 0.1 compare_and_fusion.5
  155.6 5.0 %gather_fusion = bf16[32,128,440]{2,1,0:T(8,128)(2,1)} fusion(bf16[32,128,440]{2,1,0:T(8,128)(2,1)} %get-tuple-element.169, s32[1024]{0:T(1024)S(1)} %pad_clamp_fusion.4), kind=kCustom, calls=%fused_computation.1.clone.clone.1 | custom fusion | bytes 7209088 | tf_op jit(solution)/shard_map/while/body/jit(_take)/gather | solution.py:30
  160.6 4.9 %gather_fusion.1 = bf16[32,128,440]{2,1,0:T(8,128)(2,1)} fusion(bf16[32,128,440]{2,1,0:T(8,128)(2,1)} %get-tuple-element.167, s32[1024]{0:T(1024)S(1)} %pad_clamp_fusion.5), kind=kCustom, calls=%fused_computation.clone.clone.1 | custom fusion | bytes 7209088 | tf_op jit(solution)/shard_map/while/body/jit(_take)/gather | solution.py:29
  165.5 0.7 add_compare_fusion.2
  166.1 6.1 %fusion.25 = f32[440,440]{1,0:T(8,128)S(1)} fusion(f32[440,440]{1,0:T(8,128)S(1)} %get-tuple-element.151, bf16[32,128,440]{2,1,0:T(8,128)(2,1)} %gather_fusion, pred[32]{0:T(512)(128)(4,1)S(1)} %get-tuple-element.135, bf16[32,128,440]{2,1,0:T(8,128)(2,1)} %gather_fusion.1, pred[32]{0:T(512)(128)(4,1)S(1)} %get-tuple-element.137, ...), kind=kOutput, calls=%fused_computation.13.clone.1 | convolution fusion | flops 1591571456 | bytes 8757856 | tf_op jit(solution)/shard_map/while/body/dot_general | solution.py:32
  172.3 5.0 %gather_fusion = bf16[32,128,440]{2,1,0:T(8,128)(2,1)} fusion(bf16[32,128,440]{2,1,0:T(8,128)(2,1)} %get-tuple-element.169, s32[1024]{0:T(1024)S(1)} %pad_clamp_fusion.4), kind=kCustom, calls=%fused_computation.1.clone.clone.1 | custom fusion | bytes 7209088 | tf_op jit(solution)/shard_map/while/body/jit(_take)/gather | solution.py:30
  177.3 4.9 %gather_fusion.1 = bf16[32,128,440]{2,1,0:T(8,128)(2,1)} fusion(bf16[32,128,440]{2,1,0:T(8,128)(2,1)} %get-tuple-element.167, s32[1024]{0:T(1024)S(1)} %pad_clamp_fusion.5), kind=kCustom, calls=%fused_computation.clone.clone.1 | custom fusion | bytes 7209088 | tf_op jit(solution)/shard_map/while/body/jit(_take)/gather | solution.py:29
  182.2 0.7 add_compare_fusion.2
  182.9 6.1 %fusion.25 = f32[440,440]{1,0:T(8,128)S(1)} fusion(f32[440,440]{1,0:T(8,128)S(1)} %get-tuple-element.151, bf16[32,128,440]{2,1,0:T(8,128)(2,1)} %gather_fusion, pred[32]{0:T(512)(128)(4,1)S(1)} %get-tuple-element.135, bf16[32,128,440]{2,1,0:T(8,128)(2,1)} %gather_fusion.1, pred[32]{0:T(512)(128)(4,1)S(1)} %get-tuple-element.137, ...), kind=kOutput, calls=%fused_computation.13.clone.1 | convolution fusion | flops 1591571456 | bytes 8757856 | tf_op jit(solution)/shard_map/while/body/dot_general | solution.py:32
  188.9 22.8 %fusion = f32[112,440]{1,0:T(8,128)S(1)} fusion(f32[440,440]{1,0:T(8,128)S(1)} %get-tuple-element.49), kind=kCustom, calls=%all-reduce-scatter | all-reduce-scatter fusion | flops 197121 | bytes 972032
  211.8 2.3 collective-permute-start
  214.1 0.6 dynamic-slice.4
  215.3 0.2 collective-permute-done
  215.5 0.2 concatenate.6
  215.8 0.7 constant_dynamic-slice_fusion
  216.5 75.9 %all-reduce.4.cloned.1.call-done = f32[110,440]{1,0:T(8,128)} async-done(((f32[110,440]{1,0:T(8,128)}), f32[110,440]{1,0:T(8,128)}) %all-reduce.4.cloned.1.call-update) | async-done | bytes 193616 | tf_op jit(solution)/shard_map/psum | solution.py:43
  292.4 1.1 copy.20
  293.4 20.9 %all-gather = f32[4,110,440]{1,2,0:T(8,128)S(1)} all-gather(f32[1,110,440]{1,2,0:T(8,128)S(1)} %copy.20), channel_id=1, replica_groups=mesh['row'=8,'col'=4] {'col'}, dimensions={0}, use_global_device_ids=true | all-gather | bytes 968000 | tf_op jit(solution)/shard_map/all_gather | solution.py:44
  314.4 0.4 copy.21
  314.7 1.0 reshape.125
  (28 shorter events, 0.5 us)
Async XLA Ops:
  6.5 1.6 copy-start
  6.5 107.7 %all-gather.4.cloned.1.call-start = ((), (), s32[]{:S(2)}) async-start(), calls=%async_computation | async-start | bytes 4505600 | tf_op jit(solution)/shard_map/all_gather | solution.py:16
  8.2 32.3 %copy-start.2 = (s32[1,4,440]{2,1,0:T(4,128)S(1)}, s32[1,4,440]{2,1,0:T(4,128)}, u32[]{:S(2)}) copy-start(s32[1,4,440]{2,1,0:T(4,128)} %param.16) | copy-start | bytes 21124
  8.2 32.4 %copy-start.1 = (bf16[1,4,128,440]{2,3,1,0:T(8,128)(2,1)S(1)}, bf16[1,4,128,440]{2,3,1,0:T(8,128)(2,1)}, u32[]{:S(2)}) copy-start(bf16[1,4,128,440]{2,3,1,0:T(8,128)(2,1)} %param.12) | copy-start | bytes 1351684
  40.4 108.5 %all-gather.6.cloned.1.call-start = ((), (), s32[]{:S(2)}) async-start(), calls=%async_computation.1 | async-start | bytes 4055040 | tf_op jit(solution)/shard_map/all_gather | solution.py:17
  57.4 234.9 %all-reduce.4.cloned.1.call-start = ((), (), s32[]{:S(2)}) async-start(), calls=%async_computation.2 | async-start | bytes 458752 | tf_op jit(solution)/shard_map/psum | solution.py:43
  148.9 6.6 %copy-start.3 = (s32[1,1,128]{2,1,0:T(1,128)S(1)}, s32[1,1,128]{2,1,0:T(1,128)}, u32[]{:S(2)}) copy-start(s32[1,1,128]{2,1,0:T(1,128)} %param.13) | copy-start | bytes 1540
  148.9 6.6 %copy-start.4 = (s32[1,1,128]{2,1,0:T(1,128)S(1)}, s32[1,1,128]{2,1,0:T(1,128)}, u32[]{:S(2)}) copy-start(s32[1,1,128]{2,1,0:T(1,128)} %param.14) | copy-start | bytes 1540
  155.5 58.6 %copy-start.5 = (u32[32]{0:T(128)S(1)}, u32[32]{0:T(128)}, u32[]{:S(2)}) copy-start(u32[32]{0:T(128)} %constant.104) | copy-start | bytes 388
  211.8 3.7 %collective-permute-start = (f32[6,440]{1,0:T(8,128)S(1)}, f32[6,440]{1,0:T(8,128)S(1)}, u32[]{:S(2)}, u32[]{:S(2)}) collective-permute-start(f32[6,440]{1,0:T(8,128)S(1)} %slice.8), channel_id=1, source_target_pairs={{0,1},{1,2},{2,3},{4,5},{5,6},{6,7},{8,9},{9,10},{10,11},{12,13},{... | collective-permute-start | bytes 31688
Sparse Core Ops, SparseCore 0:
  40.5 73.7 all-gather.3
  116.2 32.6 all-gather.5
  216.6 75.6 all-reduce.3
where the time goes:
time: 325 us; the launch traced here: 322 us
  waiting for transfers between devices  160 us (49%)
  local copies, waits for them, and re-layouts  83.4 us (26%)
  blocking collectives  43.7 us (13%)
  between operations  14.6 us (4%)
  matrix products  12.1 us (4%)
  other arithmetic  5.57 us (2%)
    psum x1, waiting for transfers between devices, shards(): band = lax.psum(band, 'row')  75.9 us
    all_gather x1, waiting for transfers between devices, shards(): row_seg = lax.all_gather(own_final, 'col', axis=1, tiled=True)[0]  56.1 us
    gather x4, local copies, waits for them, and re-layouts, permute_columns(): return jnp.take(blocks, orbital_map, axis=1)  46.6 us
    all_gather x1, waiting for transfers between devices, shards(): column_seg = lax.all_gather(own_initial, 'row', axis=1, tiled=True)[0]  28.2 us
    unnamed x1, blocking collectives  22.8 us
    all_gather x1, blocking collectives, shards(): density = lax.all_gather(band, 'col', axis=0, tiled=True)  20.9 us
    while x2, local copies, waits for them, and re-layouts, shards(): lax.fori_loop(0, turns, advance, jnp.zeros((orbitals, orbitals), jnp.floa...  12.9 us
    dot_general x2, matrix products, advance(): lax.dot_general(left.reshape(-1, orbitals), right.reshape(-1, orbitals),...  12.1 us
  transfers between devices with their start and end apart: 4, of which 4 were waited for; matrix products, arithmetic and copies ran while one was open for 7% of the time, Pallas kernels for 0%

commit v1 on v0

v1 whole, which is shorter than its diff:
```python
import functools

import jax
import jax.numpy as jnp
from jax import lax
from jax.experimental import pallas as pl
from jax.experimental.pallas import tpu as pltpu
from jax.sharding import PartitionSpec as P

MESH = pl.DeviceIdType.MESH
UNROLL = 4


def flip(value, bit):
    return value + bit - 2 * bit * lax.rem(lax.div(value, bit), 2)


def flip_many(value, mask):
    bit = 1
    while bit <= mask:
        if mask & bit:
            value = flip(value, bit)
        bit *= 2
    return value


def relay_plan(rows):
    bits = []
    bit = 2
    while bit < rows:
        bits.append(bit)
        bit *= 2
    plans = []
    for order in (bits, bits[::-1]):
        diffs = [(0, 0)]
        for position, bit in enumerate(order):
            diffs += [(diff | bit, position + 1) for diff, _ in list(diffs)]
        plans.append((order, diffs))
    return plans


def permute(block, orbital_map):
    orbitals = block.shape[1]
    chosen = lax.broadcasted_iota(jnp.int32, (orbitals, orbitals), 0) == orbital_map
    onehot = jnp.where(chosen, 1.0, 0.0).astype(jnp.bfloat16)
    moved = jnp.dot(block, onehot, preferred_element_type=jnp.float32)
    return moved.T.astype(jnp.bfloat16)


def spread_kernel(rows, cols, fin_ref, ini_ref, fmap_ref, imap_ref, list_ref, f_all, i_all, l_all,
                  f_own, i_own, zero, local_sem, send_sem, recv_sem, zsend, zrecv, fsend, frecv, lsend, lrecv):
    r = lax.axis_index("row")
    c = lax.axis_index("col")
    groups = cols // 2
    own_i = ini_ref.shape[0]
    own_f = fin_ref.shape[0]
    half = own_i // 2
    plans = relay_plan(rows)

    barrier = pltpu.get_barrier_semaphore()
    peers = []
    bit = 1
    while bit < rows:
        peers.append((flip(r, bit), c))
        bit *= 2
    peers += [(r, flip_many(c, mask)) for mask in [1] + [2 * g for g in range(1, groups)]]
    for peer in peers:
        pl.semaphore_signal(barrier, inc=1, device_id=peer, device_id_type=MESH)

    for j in range(own_i):
        i_own[j] = permute(ini_ref[j], imap_ref[j])
    pl.semaphore_wait(barrier, len(peers))

    sent = []

    def remote(src, dst, ssem, rsem, peer):
        copy = pltpu.make_async_remote_copy(src_ref=src, dst_ref=dst, send_sem=ssem, recv_sem=rsem,
                                            device_id=peer, device_id_type=MESH)
        copy.start()
        sent.append(copy)

    def part(h):
        return pl.ds(h * half, half)

    used = {}

    def forward(g, h, diff, position, src):
        order, _ = plans[h]
        targets = order[position:] + [1]
        for bit in targets:
            k = used.setdefault((g, h), 0)
            used[(g, h)] = k + 1
            remote(src, i_all.at[g, diff ^ bit, part(h)], send_sem.at[g, h, k], recv_sem.at[g, h, diff ^ bit],
                   (flip(r, bit), c))

    for h in range(2):
        for g in range(1, groups):
            remote(i_own.at[part(h)], i_all.at[g, 0, part(h)], zsend.at[g, h], zrecv.at[g, h], (r, flip_many(c, 2 * g)))
        forward(0, h, 0, 0, i_own.at[part(h)])
    for g in range(1, groups):
        remote(list_ref, l_all.at[g], lsend.at[g], lrecv.at[g], (r, flip_many(c, 2 * g)))

    local = [pltpu.make_async_copy(i_own, i_all.at[0, 0], local_sem.at[0]),
             pltpu.make_async_copy(list_ref, l_all.at[0], local_sem.at[1])]
    zero[...] = jnp.zeros_like(zero)
    for j in range(own_f):
        f_own[j] = permute(fin_ref[j], fmap_ref[j])
    remote(f_own, f_all.at[pl.ds(own_f, own_f)], fsend, frecv, (r, flip(c, 1)))
    local += [pltpu.make_async_copy(f_own, f_all.at[pl.ds(0, own_f)], local_sem.at[2]),
              pltpu.make_async_copy(zero, f_all.at[2 * own_f], local_sem.at[3])]
    for copy in local:
        copy.start()

    def arrived(ref, ssem, rsem):
        pltpu.make_async_remote_copy(src_ref=ref, dst_ref=ref, send_sem=ssem, recv_sem=rsem,
                                     device_id=(flip(r, 1), c), device_id_type=MESH).wait_recv()

    def relay(g, h, diff, position):
        here = i_all.at[g, diff, part(h)]
        if diff == 0:
            arrived(here, zsend.at[g, h], zrecv.at[g, h])
        else:
            arrived(here, send_sem.at[g, h, 0], recv_sem.at[g, h, diff])
        forward(g, h, diff, position, here)

    longest = len(plans[0][1])
    for wave in range(groups + longest):
        for g in range(groups):
            index = wave - g + 1
            if g == 0 and index == 0:
                continue
            for h in range(2):
                if g > 0:
                    index = wave - g
                if 0 <= index < longest:
                    diff, position = plans[h][1][index]
                    if g == 0 and diff == 0:
                        continue
                    relay(g, h, diff, position)
    for g in range(groups):
        for h in range(2):
            for diff, _ in plans[h][1]:
                arrived(i_all.at[g, diff ^ 1, part(h)], send_sem.at[g, h, 0], recv_sem.at[g, h, diff ^ 1])
    for g in range(1, groups):
        arrived(l_all.at[g], lsend.at[g], lrecv.at[g])
    arrived(f_all.at[pl.ds(own_f, own_f)], fsend, frecv)
    for copy in sent:
        copy.wait_send()
    for copy in local:
        copy.wait()


def density_kernel(rows, cols, own_f, own_i, f_ref, i_ref, l_ref, out_ref, list_f, list_i):
    r = lax.axis_index("row")
    c = lax.axis_index("col")
    groups = cols // 2
    total = jnp.int32(0)
    for g in range(groups):
        def collect(p, n):
            q = l_ref[g, 0, p]
            s = l_ref[g, 1, p]
            apart = lax.div(q, own_f) ^ c
            list_f[n] = apart * own_f + lax.rem(q, own_f)
            list_i[n] = (g * rows + (lax.div(s, own_i) ^ r)) * own_i + lax.rem(s, own_i)
            return n + jnp.where(apart < 2, 1, 0).astype(jnp.int32)

        total = lax.fori_loop(0, l_ref[g, 2, 0], collect, total)
    for k in range(UNROLL):
        list_f[total + k] = 2 * own_f
        list_i[total + k] = 0
    out_ref[...] = jnp.zeros_like(out_ref)

    def step(t, carry):
        first = t * UNROLL
        left = jnp.concatenate([f_ref[list_f[first + k]] for k in range(UNROLL)], axis=1)
        right = jnp.concatenate([i_ref[list_i[first + k]] for k in range(UNROLL)], axis=1)
        out_ref[...] += lax.dot_general(left, right, (((1,), (1,)), ((), ())), preferred_element_type=jnp.float32)
        return carry

    lax.fori_loop(0, lax.div(total + UNROLL - 1, UNROLL), step, 0)


def shards(rows, cols, final_amp, initial_amp, pair_final, pair_initial, map_final, map_initial, counts):
    own_f, blk, orb = final_amp.shape[1:]
    own_i = initial_amp.shape[1]
    slots = pair_final.shape[2]
    groups = cols // 2
    lists = jnp.concatenate([pair_final[0], pair_initial[0], jnp.broadcast_to(counts, (6, slots))], axis=0)
    vmem = pl.BlockSpec(memory_space=pltpu.VMEM)
    hbm = pl.BlockSpec(memory_space=pl.ANY)
    dma = pltpu.SemaphoreType.DMA
    f_all, i_all, l_all = pl.pallas_call(
        functools.partial(spread_kernel, rows, cols),
        out_shape=(jax.ShapeDtypeStruct((2 * own_f + 1, orb, blk), jnp.bfloat16),
                   jax.ShapeDtypeStruct((groups, rows, own_i, orb, blk), jnp.bfloat16),
                   jax.ShapeDtypeStruct((groups, 8, slots), jnp.int32)),
        in_specs=[vmem] * 5,
        out_specs=(hbm, hbm, hbm),
        scratch_shapes=[pltpu.VMEM((own_f, orb, blk), jnp.bfloat16), pltpu.VMEM((own_i, orb, blk), jnp.bfloat16),
                        pltpu.VMEM((orb, blk), jnp.bfloat16),
                        dma((4,)), dma((groups, 2, rows)), dma((groups, 2, rows)),
                        dma((groups, 2)), dma((groups, 2)), dma, dma, dma((groups,)), dma((groups,))],
        compiler_params=pltpu.CompilerParams(collective_id=0, has_side_effects=True, vmem_limit_bytes=40 << 20),
    )(final_amp[0], initial_amp[0], map_final[0][:, None], map_initial[0][:, None], lists)
    i_all = i_all.reshape(-1, orb, blk)
    partial = pl.pallas_call(
        functools.partial(density_kernel, rows, cols, own_f, own_i),
        out_shape=jax.ShapeDtypeStruct((orb, orb), jnp.float32),
        in_specs=[vmem, vmem, pl.BlockSpec(memory_space=pltpu.SMEM)],
        out_specs=vmem,
        scratch_shapes=[pltpu.SMEM((groups * slots + UNROLL,), jnp.int32)] * 2,
        compiler_params=pltpu.CompilerParams(vmem_limit_bytes=50 << 20),
    )(f_all, i_all, l_all)
    band = lax.psum_scatter(partial, "col", scatter_dimension=0, tiled=True)
    band = lax.psum(band, "row")
    return lax.all_gather(band, "col", axis=0, tiled=True)


def solution(mesh):
    placed = (
        P("row", "col", None, None),
        P("col", "row", None, None),
        P("row", "col", None),
        P("row", "col", None),
        P("row", "col", None),
        P("col", "row", None),
        P("row", "col"),
    )
    body = functools.partial(shards, mesh.shape["row"], mesh.shape["col"])
    return jax.shard_map(body, mesh=mesh, in_specs=placed, out_specs=P(), check_vma=False)
```

time: 325 us -> 174 us (0.54)
  waiting for transfers between devices: 160 us -> 51.6 us
  local copies, waits for them, and re-layouts: 83.4 us -> 11.2 us
  Pallas kernels: 0 us -> 50 us
  matrix products: 12.1 us -> 0 us
  other arithmetic: 5.57 us -> 0.74 us
    all_gather x2 -> x0, waiting for transfers between devices: 84.3 us -> none  [the longest x1 56.1 us: shards(): row_seg = lax.all_gather(own_final, 'col', axis=1, tiled=True)[0]]
    gather x8 -> x0, local copies, waits for them, and re-layouts: 66.4 us -> none  [the longest x4 46.6 us: permute_columns(): return jnp.take(blocks, orbital_map, axis=1)]
    pallas_call x0 -> x2, Pallas kernels: none -> 50 us  [the longest x1 40.8 us: shards(): pl.pallas_call(functools.partial(spread_kernel, rows, cols), out_shape=(j...]
    psum x1, waiting for transfers between devices: 75.9 us -> 51.5 us  [shards(): band = lax.psum(band, 'row')]
    while x2 -> x0, local copies, waits for them, and re-layouts: 12.9 us -> none  [shards(): lax.fori_loop(0, turns, advance, jnp.zeros((orbitals, orbitals), jnp.floa...]
    dot_general x2 -> x0, matrix products: 12.1 us -> none  [advance(): lax.dot_general(left.reshape(-1, orbitals), right.reshape(-1, orbitals),...]
    unnamed x18 -> x12, local copies, waits for them, and re-layouts: 3.68 us -> 9.29 us
  transfers between devices with their start and end apart: 4 -> 2, of which waited for: 4 -> 2; matrix products, arithmetic and copies ran while one was open for 7% -> 0% of each run, Pallas kernels for 0% -> 0%
where the time goes in v1:
time: 174 us
  waiting for transfers between devices  51.6 us (30%)
  Pallas kernels  50 us (29%)
  blocking collectives  43.8 us (25%)
  between operations  14.8 us (9%)
  local copies, waits for them, and re-layouts  11.2 us (6%)
    psum x1, waiting for transfers between devices, shards(): band = lax.psum(band, 'row')  51.5 us
    pallas_call x1, Pallas kernels, shards(): pl.pallas_call(functools.partial(spread_kernel, rows, cols), out_shape=(j...  40.8 us
    unnamed x1, blocking collectives  22.9 us
    all_gather x1, blocking collectives, shards(): return lax.all_gather(band, 'col', axis=0, tiled=True)  20.9 us
    unnamed x12, local copies, waits for them, and re-layouts  9.29 us
    pallas_call x1, Pallas kernels, shards(): pl.pallas_call(functools.partial(density_kernel, rows, cols, own_f, own_i...  9.26 us
  transfers between devices with their start and end apart: 2, of which 2 were waited for; matrix products, arithmetic and copies ran while one was open for 0% of the time, Pallas kernels for 0%

profile of v1, /device:TPU:0, one launch (start us, length us, event | category | flops | bytes accessed | tf_op | source)
XLA Modules:
  0.0 173.8 jit_solution(11773846265208078642)
XLA Ops:
  6.5 0.0 all-reduce.4.cloned.1.call-start
  6.5 1.5 copy.12
  8.0 0.0 copy-start.1
  8.0 1.2 copy.13
  9.2 0.7 broadcast_in_dim_squeeze.6.fmap_ref
  10.0 0.7 broadcast_in_dim_squeeze.7.imap_ref
  11.3 0.1 pad.2.clone
  11.4 0.7 add_add_fusion.list_ref
  12.2 40.8 %shard_map.73 = (bf16[17,440,128]{2,1,0:T(8,128)(2,1)S(1)}, bf16[2,8,4,440,128]{4,3,2,1,0:T(8,128)(2,1)S(1)}, s32[2,8,128]{2,1,0:T(8,128)S(1)}) custom-call(bf16[8,128,440]{2,1,0:T(8,128)(2,1)S(1)} %bitcast.12, bf16[4,128,440]{2,1,0:T(8,128)(2,1)S(1)} %bitcast.13, s32[8,1,440]{2,1,0:T(1,128)S(1)} %broadcast_in_dim_squeeze.6.fmap_ref, ...), custom_call_target="tpu_custom_call" | custom-call | tf_op jit(solution)/shard_map/pallas_call | solution.py:192
  52.9 0.0 copy-start
  52.9 3.0 %copy-done = bf16[2,8,4,440,128]{4,3,2,1,0:T(8,128)(2,1)} copy-done((bf16[2,8,4,440,128]{4,3,2,1,0:T(8,128)(2,1)}, bf16[2,8,4,440,128]{4,3,2,1,0:T(8,128)(2,1)S(1)}, u32[]{:S(2)}) %copy-start) | copy-done | bytes 7208984
  55.9 9.3 %shard_map.74 = f32[440,440]{1,0:T(8,128)S(1)} custom-call(bf16[17,440,128]{2,1,0:T(8,128)(2,1)S(1)} %get-tuple-element.8.f_ref, bf16[64,440,128]{2,1,0:T(8,128)(2,1)} %bitcast.11, s32[2,8,128]{2,1,0:T(8,128)S(1)} %get-tuple-element.10.l_ref), custom_call_target="tpu_custom_call" | custom-call | tf_op jit(solution)/shard_map/pallas_call | solution.py:206
  65.2 22.9 %fusion = f32[112,440]{1,0:T(8,128)S(1)} fusion(f32[440,440]{1,0:T(8,128)S(1)} %shard_map.74), kind=kCustom, calls=%all-reduce-scatter | all-reduce-scatter fusion | flops 197121 | bytes 972032
  88.0 1.6 collective-permute-start
  89.7 0.0 copy-done.1
  89.7 0.6 dynamic-slice.4
  91.0 0.2 collective-permute-done
  91.1 0.2 concatenate.4
  91.4 0.7 constant_dynamic-slice_fusion
  92.1 0.0 all-reduce.4.cloned.1.call-update
  92.1 51.5 %all-reduce.4.cloned.1.call-done = f32[110,440]{1,0:T(8,128)} async-done(((f32[110,440]{1,0:T(8,128)}), f32[110,440]{1,0:T(8,128)}) %all-reduce.4.cloned.1.call-update) | async-done | bytes 193616 | tf_op jit(solution)/shard_map/psum | solution.py:215
  143.6 1.1 copy.14
  144.7 20.9 %all-gather = f32[4,110,440]{1,2,0:T(8,128)S(1)} all-gather(f32[1,110,440]{1,2,0:T(8,128)S(1)} %copy.14), channel_id=1, replica_groups=mesh['row'=8,'col'=4] {'col'}, dimensions={0}, use_global_device_ids=true | all-gather | bytes 968000 | tf_op jit(solution)/shard_map/all_gather | solution.py:216
  165.6 0.4 copy.15
  166.0 1.0 reshape.5
  (2 shorter events, 0.0 us)
Async XLA Ops:
  6.5 137.1 %all-reduce.4.cloned.1.call-start = ((), (), s32[]{:S(2)}) async-start(), calls=%async_computation | async-start | bytes 458752 | tf_op jit(solution)/shard_map/psum | solution.py:215
  8.0 81.7 %copy-start.1 = (u32[32]{0:T(128)S(1)}, u32[32]{0:T(128)}, u32[]{:S(2)}) copy-start(u32[32]{0:T(128)} %constant.9) | copy-start | bytes 388
  52.9 3.0 %copy-start = (bf16[2,8,4,440,128]{4,3,2,1,0:T(8,128)(2,1)}, bf16[2,8,4,440,128]{4,3,2,1,0:T(8,128)(2,1)S(1)}, u32[]{:S(2)}) copy-start(bf16[2,8,4,440,128]{4,3,2,1,0:T(8,128)(2,1)S(1)} %get-tuple-element.9) | copy-start | bytes 21626884
  88.0 3.1 %collective-permute-start = (f32[6,440]{1,0:T(8,128)S(1)}, f32[6,440]{1,0:T(8,128)S(1)}, u32[]{:S(2)}, u32[]{:S(2)}) collective-permute-start(f32[6,440]{1,0:T(8,128)S(1)} %slice), channel_id=1, source_target_pairs={{0,1},{1,2},{2,3},{4,5},{5,6},{6,7},{8,9},{9,10},{10,11},{12,13},{... | collective-permute-start | bytes 31688
Sparse Core Ops, SparseCore 0:
  92.3 51.2 all-reduce.3
